TPU v7x, 768 devices: a whole 4x8x12 slice. The times are simulated.
768 devices in a mesh: section: 32 (over x_lo, y, core), dp: 24 (over z, x_hi).
Axes of the slice: x: 4 (x_hi: 2, x_lo: 2; x = x_hi * 2 + x_lo), y: 8, z: 12, core: 2. Of those that a mesh axis runs over, the one named last changes fastest.
Arguments:
- queries: bfloat16 [24576, 6144], P('section', 'dp'), may hold values from -6 to 6
- key_input: bfloat16 [24576, 6144], P('section', 'dp'), may hold values from -6 to 6
- values_in: bfloat16 [24576, 6144], P('section', 'dp'), may hold values from -6 to 6
- cotangent: bfloat16 [24576, 6144], P('section', 'dp'), may hold values from -6 to 6
- norm_gain: bfloat16 [6144], P('dp'), may hold values from 0.099609375 to 1.8984375
- decay_log: float32 [48], P('dp'), as said below
- doc_starts: int32 [24576], P('section'), may hold values 0 or 1
Outputs:
- grad_query: bfloat16 [24576, 6144], P('section', 'dp')
- grad_key: bfloat16 [24576, 6144], P('section', 'dp')
- grad_value: bfloat16 [24576, 6144], P('section', 'dp')
- grad_gain: float32 [6144], P('dp')
Inputs may be any that keep to these rules, and one draw needn't show every extreme that they name: `doc_starts`: 1 marks a token that begins a new document: no state passes into it from earlier tokens. `decay_log`: negative for every head.
All inputs are finite; a program needn't handle non-finite values. No bound on the sum of `doc_starts` on one device may be relied on, other than what follows from the above.
Results may differ from a plain program's by a relative error of at most 0.001.
Values sent between devices are 32-bit elements; how exact they have to be, the bound alone decides.
A program may use at most 64 MiB of HBM per device.

v0:
```python
import math

import jax
import jax.numpy as jnp
from jax import lax
from jax.sharding import PartitionSpec as P

epsilon = 1e-05


def carried_in(part, axis, combine, identity, reverse):
    count = lax.axis_size(axis)
    place = lax.axis_index(axis)
    ahead = count - 1 - place if reverse else place
    gathered = jax.tree.map(lambda a: lax.all_gather(a, axis), part)
    state = jax.tree.map(lambda a, e: jnp.zeros_like(a) + jnp.asarray(e, a.dtype), part, identity)

    def one(lap, state):
        source = count - 1 - lap if reverse else lap
        return combine(
            state, jax.tree.map(lambda a: lax.dynamic_index_in_dim(a, source, 0, False), gathered)
        )

    return lax.fori_loop(0, ahead, one, state)


def to_heads(array, heads):
    rows, width = array.shape
    return array.reshape(rows, heads, width // heads).transpose(1, 0, 2)


def to_rows(array):
    heads, rows, part = array.shape
    return array.transpose(1, 0, 2).reshape(rows, heads * part)


def block_factors(doc_starts, decay_log):
    count = doc_starts.shape[0]
    segment = jnp.cumsum(doc_starts)
    position = jnp.arange(1, count + 1).astype(jnp.float32)
    offset = position[:, None] - position[None, :]
    keep = (offset >= 0.0) & (segment[:, None] == segment[None, :])
    masks = jnp.where(
        keep[None], jnp.exp(decay_log[:, None, None] * jnp.maximum(offset, 0.0)[None]), 0.0
    )
    prefix = jnp.where((segment == 0)[None], jnp.exp(decay_log[:, None] * position[None]), 0.0)
    suffix = jnp.where(
        (segment == segment[-1])[None], jnp.exp(decay_log[:, None] * (count - position)[None]), 0.0
    )
    total = jnp.where(segment[-1] == 0, jnp.exp(decay_log * count), 0.0)
    return (masks, prefix, suffix, total)


def combine(earlier, later):
    return (earlier[0] * later[0], later[0][:, None, None] * earlier[1] + later[1])


def product(form, left, right):
    return jnp.einsum(form, left, right, precision=lax.Precision.HIGHEST)


def shards(queries, key_input, values_in, cotangent, norm_gain, decay_log, doc_starts):
    heads = decay_log.shape[0]
    rows = queries.shape[0]
    part = queries.shape[1] // heads
    features = heads * part * lax.axis_size("dp")
    length = rows * lax.axis_size("section")
    query_heads = to_heads(queries, heads).astype(jnp.float32)
    key_heads = to_heads(key_input, heads).astype(jnp.float32)
    value_heads = to_heads(values_in, heads).astype(jnp.float32)
    upstream = to_heads(cotangent, heads).astype(jnp.float32)
    gain_heads = norm_gain.astype(jnp.float32).reshape(heads, 1, part)
    masks, prefix, suffix, total = block_factors(doc_starts, decay_log)
    scores = masks * product("hti,hsi->hts", query_heads, key_heads)
    forward_terms = product("hsi,hsj->hij", suffix[..., None] * key_heads, value_heads)
    identity = (jnp.ones_like(total), jnp.zeros_like(forward_terms))
    state_in = carried_in((total, forward_terms), "section", combine, identity, False)[1]
    outputs = product("hts,hsj->htj", scores, value_heads) + prefix[..., None] * product(
        "hti,hij->htj", query_heads, state_in
    )
    grad_norm = upstream * gain_heads
    square_local = jnp.sum(outputs * outputs, axis=(0, 2))
    square_total = lax.psum(square_local, "dp")
    scale_rows = lax.rsqrt(square_total / features + epsilon)
    normed = outputs * scale_rows[None, :, None]
    mixed = lax.psum(jnp.sum(grad_norm * normed, axis=(0, 2)), "dp") / features
    grad_out = scale_rows[None, :, None] * (grad_norm - normed * mixed[None, :, None])
    gain_local = jnp.sum(upstream * normed, axis=1).reshape(heads * part)
    grad_gain = lax.psum(gain_local, "section") / math.sqrt(length)
    backward_terms = product("hti,htj->hij", prefix[..., None] * query_heads, grad_out)
    carry_in = carried_in((total, backward_terms), "section", combine, identity, True)[1]
    grad_scores = masks * product("htj,hsj->hts", grad_out, value_heads)
    grad_query = product("hts,hsi->hti", grad_scores, key_heads) + prefix[..., None] * product(
        "htj,hij->hti", grad_out, state_in
    )
    grad_key = product("hts,hti->hsi", grad_scores, query_heads) + suffix[..., None] * product(
        "hsj,hij->hsi", value_heads, carry_in
    )
    grad_value = product("hts,htj->hsj", scores, grad_out) + suffix[..., None] * product(
        "hsi,hij->hsj", key_heads, carry_in
    )
    return (
        to_rows(grad_query).astype(jnp.bfloat16),
        to_rows(grad_key).astype(jnp.bfloat16),
        to_rows(grad_value).astype(jnp.bfloat16),
        grad_gain,
    )


def solution(mesh):
    in_specs = (
        P("section", "dp"),
        P("section", "dp"),
        P("section", "dp"),
        P("section", "dp"),
        P("dp"),
        P("dp"),
        P("section"),
    )
    out_specs = (P("section", "dp"), P("section", "dp"), P("section", "dp"), P("dp"))
    return jax.shard_map(shards, mesh=mesh, in_specs=in_specs, out_specs=out_specs, check_vma=False)
```

profile of v0, /device:TPU:1, one launch (start us, length us, event | category | flops | bytes accessed | tf_op | source)
XLA Modules:
  0.0 431.2 jit_solution(13777550294665565801)
XLA Ops:
  7.3 1.0 reduce-window.9
  10.6 2.7 fusion.50
  14.0 1.3 dynamic-slice
  16.7 63.3 %all-reduce = f32[64]{0:T(128)S(1)} all-reduce(f32[64]{0:T(128)S(1)} %fusion.65), channel_id=2, replica_groups=mesh['section'=32,'dp'=24] {'section'}, use_global_device_ids=true, to_apply=%add | all-reduce | flops 64 | bytes 512
  80.7 1.9 copy.72
  82.6 1.2 copy.53
  83.8 1.3 bitcast_convert_fusion
  85.9 1.8 fusion.54
  87.8 2.1 copy-done.1
  89.9 4.5 %fusion.4 = f32[2,768,128]{1,2,0:T(8,128)} fusion(f32[2,768,768]{2,1,0:T(8,128)S(1)} %fusion.54, f32[768,768]{1,0:T(8,128)S(1)} %subtract_maximum_fusion, f32[2]{0:T(128)S(1)} %copy-done.12, pred[768,768]{1,0:T(8,128)(4,1)S(1)} %fusion.22, bf16[768,256]{1,0:T(8,128)(2,1)S(1)} %copy-done.8), kind=kOutput, calls=%fused_computation.8 | convolution fusion | flops 1815478272 | bytes 8847368 | tf_op jit(solution)/shard_map/hts,hsj->htj/dot_general | solution.py:59
  95.0 2.4 while.26
  95.7 1.7 bitcast_add_fusion.4
  97.4 2.8 multiply_reduce_fusion.2
  100.2 50.8 %psum.21 = f32[768]{0:T(1024)} all-reduce(f32[768]{0:T(1024)S(1)} %get-tuple-element.174), channel_id=1, replica_groups=mesh['section'=32,'dp'=24] {'dp'}, use_global_device_ids=true, to_apply=%region_5.6 | all-reduce | flops 768 | bytes 6144 | tf_op jit(solution)/shard_map/psum | solution.py:83
  151.7 2.0 multiply_reduce_fusion
  153.7 44.1 %psum.22 = f32[768]{0:T(1024)S(1)} all-reduce(f32[768]{0:T(1024)} %get-tuple-element.147), channel_id=1, replica_groups=mesh['section'=32,'dp'=24] {'dp'}, use_global_device_ids=true, to_apply=%region_7.8 | all-reduce | flops 768 | bytes 6144 | tf_op jit(solution)/shard_map/psum | solution.py:86
  197.8 1.6 subtract_multiply_fusion
  199.4 2.6 fusion.47
  202.8 3.1 fusion.53
  206.0 3.6 fusion.27
  209.7 1.6 fusion.46
  211.3 1.9 copy.59
  213.2 141.0 %psum.23 = f32[256]{0:T(256)} all-reduce(f32[256]{0:T(256)S(1)} %bitcast.152), channel_id=1, replica_groups=mesh['section'=32,'dp'=24] {'section'}, use_global_device_ids=true, to_apply=%region_11.12 | all-reduce | flops 256 | bytes 2048 | tf_op jit(solution)/shard_map/psum | solution.py:89
  354.2 1.3 broadcast_multiply_fusion.1
  355.5 6.4 %fusion.30 = f32[768,2,128]{0,2,1:T(8,128)} fusion(bf16[2,768,128]{1,2,0:T(8,128)(2,1)} %bitcast.146, f32[2,768,768]{2,1,0:T(8,128)} %copy-done.2, f32[768,768]{1,0:T(8,128)S(1)} %subtract_maximum_fusion, f32[2]{0:T(128)S(1)} %copy-done.13, pred[768,768]{1,0:T(8,128)(4,1)} %copy-done.3), kind=kOutput, calls=%fused_computation.31 | convolution fusion | flops 1815478272 | bytes 8847368 | tf_op jit(solution)/shard_map/hts,hti->hsi/dot_general | solution.py:59
  361.9 7.2 %fusion.35 = f32[768,2,128]{0,2,1:T(8,128)} fusion(f32[2,768,128]{1,2,0:T(8,128)S(1)} %subtract_multiply_fusion, f32[2,768,768]{2,1,0:T(8,128)} %copy-done.1, f32[768,768]{1,0:T(8,128)S(1)} %subtract_maximum_fusion, f32[2]{0:T(128)S(1)} %copy-done.13, pred[768,768]{1,0:T(8,128)(4,1)S(1)} %copy-done.5), kind=kOutput, calls=%fused_computation.35 | convolution fusion | flops 1815478272 | bytes 9240584 | tf_op jit(solution)/shard_map/hts,htj->hsj/dot_general | solution.py:59
  369.1 51.3 %while.27 = (s32[]{:T(128)}, f32[2,128,128]{2,1,0:T(8,128)S(1)}, s32[]{:T(128)}, f32[32,2]{1,0:T(8,128)}, f32[32,2,128,128]{3,2,1,0:T(8,128)}, /*index=5*/s32[]{:T(128)}, s32[]{:T(128)}, s32[]{:T(128)}, s32[]{:T(128)}) while((s32[]{:T(128)}, f32[2,128,128]{2,1,0:T(8,128)S(1)}, s32[]{:T(128)}, f32[32,2]{1,0:T(8,128)}, ...), condition=%wide.region_9.10_spmd, body=%wide.region_8.9_spmd.sunk | while | flops 65542 | bytes 393387 | solution.py:24
  369.9 1.0 bitcast_add_fusion.5
  371.6 1.0 bitcast_add_fusion.5
  373.3 1.0 bitcast_add_fusion.5
  380.2 1.0 bitcast_add_fusion.5
  420.4 1.7 fusion.45
  (118 shorter events, 56.4 us)
Async XLA Ops:
  7.2 3.4 copy-start
  7.2 87.2 %all-gather.6.cloned.1.call-start = ((), (), s32[]{:S(2)}) async-start(), calls=%async_computation | async-start | bytes 4325376 | tf_op jit(solution)/shard_map/all_gather | solution.py:15
  7.2 77.8 %copy-start.11 = (f32[768]{0:T(1024)}, f32[768]{0:T(1024)S(1)}, u32[]{:S(2)}) copy-start(f32[768]{0:T(1024)S(1)} %broadcast_subtract_fusion) | copy-start | bytes 9220
  8.6 76.5 %copy-start.14 = (pred[768]{0:T(1024)(128)(4,1)}, pred[768]{0:T(1024)(128)(4,1)S(1)}, u32[]{:S(2)}) copy-start(pred[768]{0:T(1024)(128)(4,1)S(1)} %get-tuple-element.168) | copy-start | bytes 2308
  9.8 75.3 %copy-start.15 = (pred[768]{0:T(1024)(128)(4,1)}, pred[768]{0:T(1024)(128)(4,1)S(1)}, u32[]{:S(2)}) copy-start(pred[768]{0:T(1024)(128)(4,1)S(1)} %broadcast_compare_fusion) | copy-start | bytes 2308
  13.3 355.8 %all-gather.8.cloned.1.call-start = ((), (), s32[]{:S(2)}) async-start(), calls=%async_computation.1 | async-start | bytes 4325376 | tf_op jit(solution)/shard_map/all_gather | solution.py:15
  82.6 7.3 %copy-start.12 = (f32[2]{0:T(128)S(1)}, f32[2]{0:T(128)}, u32[]{:S(2)}) copy-start(f32[2]{0:T(128)} %param.16) | copy-start | bytes 28
  83.8 67.9 %copy-start.6 = (f32[768,256]{0,1:T(8,128)}, f32[768,256]{0,1:T(8,128)S(1)}, u32[]{:S(2)}) copy-start(f32[768,256]{0,1:T(8,128)S(1)} %copy.53) | copy-start | bytes 2359300
  83.8 6.1 %copy-start.8 = (bf16[768,256]{1,0:T(8,128)(2,1)S(1)}, bf16[768,256]{1,0:T(8,128)(2,1)}, u32[]{:S(2)}) copy-start(bf16[768,256]{1,0:T(8,128)(2,1)} %param.13) | copy-start | bytes 1179652
  85.7 2.1 copy-start.3
  87.8 2.1 copy-start.1
  199.4 6.6 %copy-start.13 = (f32[2]{0:T(128)S(1)}, f32[2]{0:T(128)}, u32[]{:S(2)}) copy-start(f32[2]{0:T(128)} %param.16) | copy-start | bytes 28
  202.0 4.0 copy-start.4
  206.0 5.3 %copy-start.2 = (f32[2,768,768]{2,1,0:T(8,128)}, f32[2,768,768]{2,1,0:T(8,128)S(1)}, u32[]{:S(2)}) copy-start(f32[2,768,768]{2,1,0:T(8,128)S(1)} %fusion.53) | copy-start | bytes 14155780
  206.0 3.7 copy-start.7
  206.0 7.2 %copy-start.16 = (f32[2,128]{1,0:T(2,128)S(1)}, f32[2,128]{1,0:T(2,128)}, u32[]{:S(2)}) copy-start(f32[2,128]{1,0:T(2,128)} %get-tuple-element.146) | copy-start | bytes 3076
  354.2 7.7 %copy-start.5 = (pred[768,768]{1,0:T(8,128)(4,1)S(1)}, pred[768,768]{1,0:T(8,128)(4,1)}, u32[]{:S(2)}) copy-start(pred[768,768]{1,0:T(8,128)(4,1)} %copy-done.3) | copy-start | bytes 1769476
  369.1 53.9 %copy-start.9 = (bf16[768,256]{1,0:T(8,128)(2,1)S(1)}, bf16[768,256]{1,0:T(8,128)(2,1)}, u32[]{:S(2)}) copy-start(bf16[768,256]{1,0:T(8,128)(2,1)} %param.13) | copy-start | bytes 1179652
  369.1 53.9 %copy-start.10 = (f32[768,2,128]{0,2,1:T(8,128)S(1)}, f32[768,2,128]{0,2,1:T(8,128)}, u32[]{:S(2)}) copy-start(f32[768,2,128]{0,2,1:T(8,128)} %fusion.30) | copy-start | bytes 2359300
Sparse Core Ops, SparseCore 0:
  13.4 80.3 all-gather.5
  202.1 155.1 all-gather.7
where the time goes:
time: 435 us; the launch traced here: 431 us
  blocking collectives  299 us (69%)
  other arithmetic  43.1 us (10%)
  matrix products  38.4 us (9%)
  local copies, waits for them, and re-layouts  33.9 us (8%)
  between operations  15.6 us (4%)
    psum x1, blocking collectives, shards(): grad_gain = lax.psum(gain_local, 'section') / math.sqrt(length)  141 us
    unnamed x1, blocking collectives  63.3 us
    psum x1, blocking collectives, shards(): square_total = lax.psum(square_local, 'dp')  50.8 us
    psum x1, blocking collectives, shards(): mixed = lax.psum(jnp.sum(grad_norm * normed, axis=(0, 2)), 'dp') / features  44.1 us
    dot_general x12, matrix products, product(): return jnp.einsum(form, left, right, precision=lax.Precision.HIGHEST)  38.4 us
    add x31, other arithmetic, combine(): later[0][:, None, None] * earlier[1] + later[1]  31.4 us
    mul x31, local copies, waits for them, and re-layouts, combine(): later[0][:, None, None] * earlier[1] + later[1]  21.4 us
  transfers between devices with their start and end apart: 2, of which 0 were waited for; matrix products, arithmetic and copies ran while one was open for 9% of the time, Pallas kernels for 0%

commit v1 on v0

v1 whole, which is shorter than its diff:
```python
import functools
import math

import jax
import jax.numpy as jnp
from jax import lax
from jax.experimental import pallas as pl
from jax.experimental.pallas import tpu as pltpu
from jax.sharding import PartitionSpec as P

epsilon = 1e-05
MESH = pl.DeviceIdType.MESH
f32 = jnp.float32
bf16 = jnp.bfloat16


def split(x):
    hi = x.astype(bf16)
    return hi, (x - hi.astype(f32)).astype(bf16)


def nn(a, b):
    return lax.dot_general(a, b, (((1,), (0,)), ((), ())), preferred_element_type=f32)


def nt(a, b):
    return lax.dot_general(a, b, (((1,), (1,)), ((), ())), preferred_element_type=f32)


def tn(a, b):
    return lax.dot_general(a, b, (((0,), (0,)), ((), ())), preferred_element_type=f32)


def wide(*parts):
    return jnp.concatenate(parts, axis=1)


def column(row):
    return jnp.transpose(jnp.broadcast_to(row, (128, row.shape[1])))


def kernel(
    sections, columns, rows, block,
    q_ref, k_ref, v_ref, g_ref, gain_ref, decay_ref, doc_ref,
    gq_ref, gk_ref, gv_ref, gg_ref,
    flag_out, flag_in,
    f_out, f_in, p_out, state,
    b_out, b_in, c_out, carry,
    gain_out, gain_in,
    pair_out, pair_in, line_out, line_in,
    pre, suf, mask, s_hi, s_lo, o, d_hi, d_lo,
    send_sem, recv_sem,
):
    me = lax.axis_index("section")
    dp = lax.axis_index("dp")
    tiers = columns // 2
    x_at = dp % 2
    z_at = dp // 2
    half = sections // 2
    depth = 256 // sections
    features = 256 * columns
    blocks = rows // block

    def to_section(source, target, which, peer):
        return pltpu.make_async_remote_copy(
            src_ref=source, dst_ref=target, send_sem=send_sem.at[which],
            recv_sem=recv_sem.at[which], device_id={"section": peer}, device_id_type=MESH,
        )

    def to_column(source, target, which, peer):
        return pltpu.make_async_remote_copy(
            src_ref=source, dst_ref=target, send_sem=send_sem.at[which],
            recv_sem=recv_sem.at[which], device_id={"dp": peer}, device_id_type=MESH,
        )

    def spread(source_of, target, which):
        def one(step, _):
            peer = (me + step) % sections
            to_section(source_of(peer), target.at[me], which, peer).start()
            return 0

        lax.fori_loop(1, sections, one, 0)

    def all_but_one(buffer, which):
        part = buffer.at[pl.ds(0, sections - 1)]
        return to_section(part, part, which, (me + 1) % sections)

    barrier = pltpu.get_barrier_semaphore()

    def greet(step, _):
        pl.semaphore_signal(
            barrier, inc=1, device_id={"section": (me + step) % sections}, device_id_type=MESH
        )
        return 0

    def greet_line(step, _):
        pl.semaphore_signal(
            barrier, inc=1, device_id={"dp": ((z_at + step) % tiers) * 2 + x_at},
            device_id_type=MESH,
        )
        return 0

    lax.fori_loop(1, sections, greet, 0)
    other = z_at * 2 + (1 - x_at)
    pl.semaphore_signal(barrier, inc=1, device_id={"dp": other}, device_id_type=MESH)
    lax.fori_loop(1, tiers, greet_line, 0)

    docs = jnp.broadcast_to(doc_ref[...].astype(f32), (8, rows)).astype(bf16)
    upper = (
        lax.broadcasted_iota(jnp.int32, (128, 128), 0)
        <= lax.broadcasted_iota(jnp.int32, (128, 128), 1)
    ).astype(f32).astype(bf16)
    run = jnp.zeros((8, 1), f32)
    parts = []
    for at in range(rows // 128):
        part = nn(docs[:, at * 128 : (at + 1) * 128], upper) + run
        run = part[:, 127:128]
        parts.append(part)
    seg_row = wide(*parts)[0:1]
    last = run[0:1]
    seg = column(seg_row)
    position = lax.broadcasted_iota(jnp.int32, (rows, 128), 0).astype(f32) + 1.0

    def head_slice(h):
        return pl.ds(pl.multiple_of(h * 128, 128), 128)

    def local_states(h, _):
        decay = decay_ref[h]
        suffix = jnp.where(seg == last, jnp.exp(decay * (rows - position)), 0.0)
        prefix = jnp.where(seg == 0.0, jnp.exp(decay * position), 0.0)
        suf[h] = suffix
        pre[h] = prefix
        hi, lo = split(suffix * k_ref[:, head_slice(h)].astype(f32))
        both = tn(wide(hi, lo), v_ref[:, head_slice(h)])
        f_out[pl.ds(h * half, half)] = (both[0:128] + both[128:256]).reshape(half, depth, 128)
        return 0

    lax.fori_loop(0, 2, local_states, 0)
    flag = jnp.broadcast_to(jnp.where(last == 0.0, 1.0, 0.0), (1, 128))
    flag_out[...] = flag
    flag_in[me] = flag
    f_in[me] = f_out[me]

    pl.semaphore_wait(barrier, sections + tiers - 1)
    spread(lambda peer: f_out.at[peer], f_in, 0)
    spread(lambda peer: flag_out, flag_in, 1)

    def pairs(h, body):
        for at in range(blocks):
            for past in range(at + 1):
                body(h, at, past)

    def forward_pair(h, at, past):
        ti, si = pl.ds(at * block, block), pl.ds(past * block, block)
        offset = (
            lax.broadcasted_iota(jnp.int32, (block, block), 0)
            - lax.broadcasted_iota(jnp.int32, (block, block), 1)
            + (at - past) * block
        )
        here = seg[at * block : (at + 1) * block]
        keep = wide(here, here) == seg_row[:, past * block : (past + 1) * block]
        if at == past:
            keep = keep & (offset >= 0)
        weights = jnp.where(
            keep, jnp.exp(decay_ref[h] * jnp.maximum(offset, 0).astype(f32)), 0.0
        )
        mask[h, ti, si] = weights
        hi, lo = split(weights * nt(q_ref[ti, head_slice(h)], k_ref[si, head_slice(h)]))
        s_hi[h, ti, si] = hi
        s_lo[h, ti, si] = lo
        values = v_ref[si, head_slice(h)]
        term = nn(hi, values) + nn(lo, values)
        if past == 0:
            o[ti, head_slice(h)] = term
        else:
            o[ti, head_slice(h)] += term

    def forward_head(h, _):
        pairs(h, forward_pair)
        return 0

    lax.fori_loop(0, 2, forward_head, 0)

    def factors():
        rate = jnp.where(me < half, decay_ref[0], decay_ref[1])
        return jnp.exp(jnp.full((depth, 128), rate * rows, f32))

    all_but_one(f_in, 0).wait_recv()
    all_but_one(flag_in, 1).wait_recv()
    total = factors()
    held = jnp.zeros((depth, 128), f32)
    for at in range(sections):
        p_out[at] = held
        held = total * flag_in[at] * held + f_in[at]
    spread(lambda peer: p_out.at[peer], state, 2)
    state[me] = p_out[me]
    all_but_one(state, 2).wait_recv()

    def state_of(buffer, h):
        return split(buffer[pl.ds(h * half, half)].reshape(128, 128))

    def finish_outputs(h, _):
        hi, lo = state_of(state, h)
        both = nn(q_ref[:, head_slice(h)], wide(hi, lo))
        o[:, head_slice(h)] += pre[h] * (both[:, 0:128] + both[:, 128:256])
        return 0

    lax.fori_loop(0, 2, finish_outputs, 0)
    outputs = o[...]
    upstream = g_ref[...].astype(f32)
    grad_norm = upstream * gain_ref[...].astype(f32)
    squares = outputs * outputs
    mixes = grad_norm * outputs
    pair_out[0:1] = jnp.sum(jnp.transpose(squares[:, 0:128] + squares[:, 128:256]), 0, keepdims=True)
    pair_out[1:2] = jnp.sum(jnp.transpose(mixes[:, 0:128] + mixes[:, 128:256]), 0, keepdims=True)
    swap = to_column(pair_out, pair_in, 3, other)
    swap.start()
    swap.wait_recv()
    line = pair_out[...] + pair_in[...]
    line_out[...] = line
    line_in[z_at] = line

    def one_tier(step, _):
        peer = ((z_at + step) % tiers) * 2 + x_at
        to_column(line_out, line_in.at[z_at], 4, peer).start()
        return 0

    lax.fori_loop(1, tiers, one_tier, 0)
    tier_part = line_in.at[pl.ds(0, tiers - 1)]
    tier_wait = to_column(tier_part, tier_part, 4, other)
    tier_wait.wait_recv()
    sums = line_in[0]
    for at in range(1, tiers):
        sums = sums + line_in[at]
    scale = lax.rsqrt(sums[0:1] / features + epsilon)
    mixed = scale * sums[1:2] / features
    scale = column(scale)
    mixed = column(mixed)
    scale = wide(scale, scale)
    normed = outputs * scale
    grad_out = scale * (grad_norm - normed * wide(mixed, mixed))
    hi, lo = split(grad_out)
    d_hi[...] = hi
    d_lo[...] = lo
    gains = jnp.sum(upstream * normed, 0, keepdims=True)
    gain_out[0:1] = gains[:, 0:128]
    gain_out[1:2] = gains[:, 128:256]

    def backward_states(h, _):
        hi, lo = split(pre[h] * q_ref[:, head_slice(h)].astype(f32))
        four = tn(wide(hi, lo), wide(d_hi[:, head_slice(h)], d_lo[:, head_slice(h)]))
        top = four[0:128] + four[128:256]
        b_out[pl.ds(h * half, half)] = (top[:, 0:128] + top[:, 128:256]).reshape(half, depth, 128)
        return 0

    lax.fori_loop(0, 2, backward_states, 0)
    b_in[me] = b_out[me]
    gain_in[me] = gain_out[...]
    spread(lambda peer: b_out.at[peer], b_in, 5)
    spread(lambda peer: gain_out, gain_in, 6)

    def start_query(h, _):
        hi, lo = state_of(state, h)
        stack = jnp.concatenate([wide(hi, hi), wide(lo, lo)], axis=0)
        both = nt(wide(d_hi[:, head_slice(h)], d_lo[:, head_slice(h)]), stack)
        gq_ref[:, head_slice(h)] = pre[h] * (both[:, 0:128] + both[:, 128:256])
        return 0

    lax.fori_loop(0, 2, start_query, 0)

    all_but_one(b_in, 5).wait_recv()
    held = jnp.zeros((depth, 128), f32)
    for at in reversed(range(sections)):
        c_out[at] = held
        held = total * flag_in[at] * held + b_in[at]
    spread(lambda peer: c_out.at[peer], carry, 7)
    carry[me] = c_out[me]

    def backward_pair(h, at, past):
        ti, si = pl.ds(at * block, block), pl.ds(past * block, block)
        grads = wide(d_hi[ti, head_slice(h)], d_lo[ti, head_slice(h)])
        values = v_ref[si, head_slice(h)]
        hi, lo = split(mask[h, ti, si] * nt(grads, wide(values, values)))
        keys = k_ref[si, head_slice(h)]
        queries = q_ref[ti, head_slice(h)]
        gq_ref[ti, head_slice(h)] += nn(hi, keys) + nn(lo, keys)
        key_term = tn(hi, queries) + tn(lo, queries)
        both = tn(s_hi[h, ti, si], grads) + tn(s_lo[h, ti, si], grads)
        value_term = both[:, 0:128] + both[:, 128:256]
        if at == past:
            gk_ref[si, head_slice(h)] = key_term
            gv_ref[si, head_slice(h)] = value_term
        else:
            gk_ref[si, head_slice(h)] += key_term
            gv_ref[si, head_slice(h)] += value_term

    def backward_head(h, _):
        pairs(h, backward_pair)
        return 0

    lax.fori_loop(0, 2, backward_head, 0)
    all_but_one(gain_in, 6).wait_recv()
    gains = gain_in[0]
    for at in range(1, sections):
        gains = gains + gain_in[at]
    gg_ref[...] = gains / math.sqrt(rows * sections)
    all_but_one(carry, 7).wait_recv()

    def finish(h, _):
        hi, lo = state_of(carry, h)
        both = nt(v_ref[:, head_slice(h)], jnp.concatenate([hi, lo], axis=0))
        gk_ref[:, head_slice(h)] += suf[h] * (both[:, 0:128] + both[:, 128:256])
        both = nn(k_ref[:, head_slice(h)], wide(hi, lo))
        gv_ref[:, head_slice(h)] += suf[h] * (both[:, 0:128] + both[:, 128:256])
        return 0

    lax.fori_loop(0, 2, finish, 0)
    all_but_one(f_in, 0).wait_send()
    all_but_one(flag_in, 1).wait_send()
    all_but_one(state, 2).wait_send()
    swap.wait_send()
    tier_wait.wait_send()
    all_but_one(b_in, 5).wait_send()
    all_but_one(gain_in, 6).wait_send()
    all_but_one(carry, 7).wait_send()


def shards(queries, key_input, values_in, cotangent, norm_gain, decay_log, doc_starts):
    rows, width = queries.shape
    sections = lax.axis_size("section")
    columns = lax.axis_size("dp")
    depth = width // sections
    tiers = columns // 2
    vmem = pl.BlockSpec(memory_space=pltpu.VMEM)
    pieces = pltpu.VMEM((sections, depth, 128), f32)
    outs = pl.pallas_call(
        functools.partial(kernel, sections, columns, rows, 256),
        out_shape=[jax.ShapeDtypeStruct((rows, width), f32)] * 3
        + [jax.ShapeDtypeStruct((2, 128), f32)],
        in_specs=[vmem] * 5 + [pl.BlockSpec(memory_space=pltpu.SMEM), vmem],
        out_specs=[vmem] * 4,
        scratch_shapes=[
            pltpu.VMEM((1, 128), f32), pltpu.VMEM((sections, 1, 128), f32),
            pieces, pieces, pieces, pieces,
            pieces, pieces, pieces, pieces,
            pltpu.VMEM((2, 128), f32), pltpu.VMEM((sections, 2, 128), f32),
            pltpu.VMEM((2, rows), f32), pltpu.VMEM((2, rows), f32),
            pltpu.VMEM((2, rows), f32), pltpu.VMEM((tiers, 2, rows), f32),
            pltpu.VMEM((2, rows, 128), f32), pltpu.VMEM((2, rows, 128), f32),
            pltpu.VMEM((2, rows, rows), f32),
            pltpu.VMEM((2, rows, rows), bf16), pltpu.VMEM((2, rows, rows), bf16),
            pltpu.VMEM((rows, width), f32),
            pltpu.VMEM((rows, width), bf16), pltpu.VMEM((rows, width), bf16),
            pltpu.SemaphoreType.DMA((8,)), pltpu.SemaphoreType.DMA((8,)),
        ],
        compiler_params=pltpu.CompilerParams(
            collective_id=0, has_side_effects=True, vmem_limit_bytes=48 * 1024 * 1024
        ),
        name="layer_grads",
    )(
        queries, key_input, values_in, cotangent, norm_gain.reshape(1, width), decay_log,
        doc_starts.reshape(1, rows),
    )
    return (
        outs[0].astype(bf16), outs[1].astype(bf16), outs[2].astype(bf16), outs[3].reshape(width),
    )


def solution(mesh):
    in_specs = (
        P("section", "dp"),
        P("section", "dp"),
        P("section", "dp"),
        P("section", "dp"),
        P("dp"),
        P("dp"),
        P("section"),
    )
    out_specs = (P("section", "dp"), P("section", "dp"), P("section", "dp"), P("dp"))
    return jax.shard_map(shards, mesh=mesh, in_specs=in_specs, out_specs=out_specs, check_vma=False)
```

time: 435 us -> 68.2 us (0.16)
  blocking collectives: 299 us -> 0 us
  Pallas kernels: 0 us -> 59 us
  other arithmetic: 43.1 us -> 2.36 us
  matrix products: 38.4 us -> 0 us
  local copies, waits for them, and re-layouts: 33.9 us -> 5.91 us
  between operations: 15.6 us -> 0.65 us
    psum x3 -> x0, blocking collectives: 236 us -> none  [the longest x1 141 us: shards(): grad_gain = lax.psum(gain_local, 'section') / math.sqrt(length)]
    unnamed x1 -> x0, blocking collectives: 63.3 us -> none
    pallas_call x0 -> x1, Pallas kernels: none -> 59 us  [shards(): pl.pallas_call(functools.partial(kernel, sections, columns, rows, 256), o...]
    dot_general x12 -> x0, matrix products: 38.4 us -> none  [product(): return jnp.einsum(form, left, right, precision=lax.Precision.HIGHEST)]
    add x31 -> x0, other arithmetic: 31.4 us -> none  [combine(): later[0][:, None, None] * earlier[1] + later[1]]
    mul x31 -> x0, local copies, waits for them, and re-layouts: 21.4 us -> none  [combine(): later[0][:, None, None] * earlier[1] + later[1]]
  transfers between devices with their start and end apart: 2 -> 0, of which waited for: 0 -> 0; matrix products, arithmetic and copies ran while one was open for 9% -> 0% of each run, Pallas kernels for 0% -> 0%
where the time goes in v1:
time: 68.2 us; the launch traced here: 67.9 us
  Pallas kernels  59 us (87%)
  local copies, waits for them, and re-layouts  5.91 us (9%)
  other arithmetic  2.36 us (3%)
    pallas_call x1, Pallas kernels, shards(): pl.pallas_call(functools.partial(kernel, sections, columns, rows, 256), o...  59 us
    unnamed x11, local copies, waits for them, and re-layouts  4.55 us

profile of v1, /device:TPU:1, one launch (start us, length us, event | category | flops | bytes accessed | tf_op | source)
XLA Modules:
  0.0 67.9 jit_solution(15594061384933346516)
XLA Ops:
  0.6 0.7 reshape.17.gain_ref
  1.3 0.0 copy-start.4
  1.3 0.7 %reshape.18.doc_ref = s32[1,768]{1,0:T(1,128)S(1)} reshape(s32[768]{0:T(1024)} %param.13) | data formatting | bytes 6144 | tf_op jit(solution)/shard_map/reshape | solution.py:362
  2.0 0.0 copy-done.4
  2.0 0.0 copy-start
  2.0 1.0 %copy-done = bf16[768,256]{1,0:T(8,128)(2,1)S(1)} copy-done((bf16[768,256]{1,0:T(8,128)(2,1)S(1)}, bf16[768,256]{1,0:T(8,128)(2,1)}, u32[]{:S(2)}) %copy-start) | copy-done | bytes 393240
  3.0 0.0 copy-start.1
  3.0 1.0 %copy-done.1 = bf16[768,256]{1,0:T(8,128)(2,1)S(1)} copy-done((bf16[768,256]{1,0:T(8,128)(2,1)S(1)}, bf16[768,256]{1,0:T(8,128)(2,1)}, u32[]{:S(2)}) %copy-start.1) | copy-done | bytes 393240
  4.0 0.0 copy-start.2
  4.0 1.0 %copy-done.2 = bf16[768,256]{1,0:T(8,128)(2,1)S(1)} copy-done((bf16[768,256]{1,0:T(8,128)(2,1)S(1)}, bf16[768,256]{1,0:T(8,128)(2,1)}, u32[]{:S(2)}) %copy-start.2) | copy-done | bytes 393240
  5.0 0.0 copy-start.3
  5.0 1.0 %copy-done.3 = bf16[768,256]{1,0:T(8,128)(2,1)S(1)} copy-done((bf16[768,256]{1,0:T(8,128)(2,1)S(1)}, bf16[768,256]{1,0:T(8,128)(2,1)}, u32[]{:S(2)}) %copy-start.3) | copy-done | bytes 393240
  6.0 59.0 %layer_grads.1 = (f32[768,256]{1,0:T(8,128)S(1)}, f32[768,256]{1,0:T(8,128)S(1)}, f32[768,256]{1,0:T(8,128)S(1)}, f32[2,128]{1,0:T(2,128)S(1)}) custom-call(bf16[768,256]{1,0:T(8,128)(2,1)S(1)} %copy-done, bf16[768,256]{1,0:T(8,128)(2,1)S(1)} %copy-done.1, bf16[768,256]{1,0:T(8,128)(2,1)S(1)} %copy-done.2, bf16[768,256]{1,0:T(8,128)(2,1)S(1)} %copy-done.3, ...), custom_call_target="tpu_custom_call" | custom-call | tf_op jit(solution)/shard_map/layer_grads/pallas_call | solution.py:336
  64.9 0.8 %convert_element_type.9 = bf16[768,256]{1,0:T(8,128)(2,1)} convert(f32[768,256]{1,0:T(8,128)S(1)} %get-tuple-element.8) | non-fusion elementwise | flops 196608 | bytes 1179648 | tf_op jit(solution)/shard_map/convert_element_type | solution.py:365
  65.7 0.8 %convert_element_type.10 = bf16[768,256]{1,0:T(8,128)(2,1)} convert(f32[768,256]{1,0:T(8,128)S(1)} %get-tuple-element.9) | non-fusion elementwise | flops 196608 | bytes 1179648 | tf_op jit(solution)/shard_map/convert_element_type | solution.py:365
  66.5 0.8 %convert_element_type.11 = bf16[768,256]{1,0:T(8,128)(2,1)} convert(f32[768,256]{1,0:T(8,128)S(1)} %get-tuple-element.10) | non-fusion elementwise | flops 196608 | bytes 1179648 | tf_op jit(solution)/shard_map/convert_element_type | solution.py:365
  67.3 0.6 copy.12
Async XLA Ops:
  1.3 0.7 %copy-start.4 = (f32[2]{0:T(128)S(1)}, f32[2]{0:T(128)}, u32[]{:S(2)}) copy-start(f32[2]{0:T(128)} %decay_ref.1) | copy-start | bytes 28
  2.0 1.0 %copy-start = (bf16[768,256]{1,0:T(8,128)(2,1)S(1)}, bf16[768,256]{1,0:T(8,128)(2,1)}, u32[]{:S(2)}) copy-start(bf16[768,256]{1,0:T(8,128)(2,1)} %q_ref.1) | copy-start | bytes 1179652
  3.0 1.0 %copy-start.1 = (bf16[768,256]{1,0:T(8,128)(2,1)S(1)}, bf16[768,256]{1,0:T(8,128)(2,1)}, u32[]{:S(2)}) copy-start(bf16[768,256]{1,0:T(8,128)(2,1)} %k_ref.1) | copy-start | bytes 1179652
  4.0 1.0 %copy-start.2 = (bf16[768,256]{1,0:T(8,128)(2,1)S(1)}, bf16[768,256]{1,0:T(8,128)(2,1)}, u32[]{:S(2)}) copy-start(bf16[768,256]{1,0:T(8,128)(2,1)} %v_ref.1) | copy-start | bytes 1179652
  5.0 1.0 %copy-start.3 = (bf16[768,256]{1,0:T(8,128)(2,1)S(1)}, bf16[768,256]{1,0:T(8,128)(2,1)}, u32[]{:S(2)}) copy-start(bf16[768,256]{1,0:T(8,128)(2,1)} %g_ref.1) | copy-start | bytes 1179652

commit v2 on v1

--- a/solution.py
+++ b/solution.py
@@ -41,9 +41,9 @@
 
 def kernel(
     sections, columns, rows, block,
-    q_ref, k_ref, v_ref, g_ref, gain_ref, decay_ref, doc_ref,
+    q_hbm, k_hbm, v_hbm, g_hbm, gain_hbm, decay_ref, doc_hbm,
     gq_ref, gk_ref, gv_ref, gg_ref,
-    flag_out, flag_in,
+    q_ref, k_ref, v_ref, g_ref, gain_ref, doc_ref, local_sem,
     f_out, f_in, p_out, state,
     b_out, b_in, c_out, carry,
     gain_out, gain_in,
@@ -60,6 +60,7 @@
     depth = 256 // sections
     features = 256 * columns
     blocks = rows // block
+    pending = []
 
     def to_section(source, target, which, peer):
         return pltpu.make_async_remote_copy(
@@ -73,17 +74,38 @@
             recv_sem=recv_sem.at[which], device_id={"dp": peer}, device_id_type=MESH,
         )
 
+    tall = sections // 4
+    hops = sorted(range(tall), key=lambda y: -min(y, tall - y))
+    steps = [
+        (x, y, c) for y in hops for x in (1, 0) for c in (1, 0) if (x, y, c) != (0, 0, 0)
+    ]
+
+    def peer_at(x, y, c):
+        return (
+            ((me // (2 * tall) + x) % 2) * (2 * tall)
+            + ((me // 2 + y) % tall) * 2
+            + (me + c) % 2
+        )
+
     def spread(source_of, target, which):
-        def one(step, _):
-            peer = (me + step) % sections
+        for step in steps:
+            peer = peer_at(*step)
             to_section(source_of(peer), target.at[me], which, peer).start()
-            return 0
-
-        lax.fori_loop(1, sections, one, 0)
 
     def all_but_one(buffer, which):
         part = buffer.at[pl.ds(0, sections - 1)]
         return to_section(part, part, which, (me + 1) % sections)
+
+    loads = []
+    for at, (source, target) in enumerate(
+        [
+            (doc_hbm, doc_ref), (k_hbm, k_ref), (v_hbm, v_ref),
+            (q_hbm, q_ref), (g_hbm, g_ref), (gain_hbm, gain_ref),
+        ]
+    ):
+        load = pltpu.make_async_copy(source, target, local_sem.at[at])
+        load.start()
+        loads.append(load)
 
     barrier = pltpu.get_barrier_semaphore()
 
@@ -105,7 +127,7 @@
     pl.semaphore_signal(barrier, inc=1, device_id={"dp": other}, device_id_type=MESH)
     lax.fori_loop(1, tiers, greet_line, 0)
 
-    docs = jnp.broadcast_to(doc_ref[...].astype(f32), (8, rows)).astype(bf16)
+    loads[0].wait()
     upper = (
         lax.broadcasted_iota(jnp.int32, (128, 128), 0)
         <= lax.broadcasted_iota(jnp.int32, (128, 128), 1)
@@ -113,7 +135,8 @@
     run = jnp.zeros((8, 1), f32)
     parts = []
     for at in range(rows // 128):
-        part = nn(docs[:, at * 128 : (at + 1) * 128], upper) + run
+        docs = doc_ref[pl.ds(at * 128, 128)].astype(f32)
+        part = nn(jnp.broadcast_to(docs[None, :], (8, 128)).astype(bf16), upper) + run
         run = part[:, 127:128]
         parts.append(part)
     seg_row = wide(*parts)[0:1]
@@ -132,18 +155,20 @@
         pre[h] = prefix
         hi, lo = split(suffix * k_ref[:, head_slice(h)].astype(f32))
         both = tn(wide(hi, lo), v_ref[:, head_slice(h)])
-        f_out[pl.ds(h * half, half)] = (both[0:128] + both[128:256]).reshape(half, depth, 128)
-        return 0
-
+        f_out[pl.ds(h * half, half), 0:depth] = (both[0:128] + both[128:256]).reshape(half, depth, 128)
+        return 0
+
+    f_out[:, depth : depth + 1] = jnp.broadcast_to(
+        jnp.where(last == 0.0, 1.0, 0.0)[None], (sections, 1, 128)
+    )
+    loads[1].wait()
+    loads[2].wait()
     lax.fori_loop(0, 2, local_states, 0)
-    flag = jnp.broadcast_to(jnp.where(last == 0.0, 1.0, 0.0), (1, 128))
-    flag_out[...] = flag
-    flag_in[me] = flag
     f_in[me] = f_out[me]
 
     pl.semaphore_wait(barrier, sections + tiers - 1)
     spread(lambda peer: f_out.at[peer], f_in, 0)
-    spread(lambda peer: flag_out, flag_in, 1)
+    pending.append(all_but_one(f_in, 0))
 
     def pairs(h, body):
         for at in range(blocks):
@@ -179,21 +204,23 @@
         pairs(h, forward_pair)
         return 0
 
-    lax.fori_loop(0, 2, forward_head, 0)
+    loads[3].wait()
+    lax.fori_loop(0, 1, forward_head, 0)
 
     def factors():
         rate = jnp.where(me < half, decay_ref[0], decay_ref[1])
         return jnp.exp(jnp.full((depth, 128), rate * rows, f32))
 
     all_but_one(f_in, 0).wait_recv()
-    all_but_one(flag_in, 1).wait_recv()
     total = factors()
     held = jnp.zeros((depth, 128), f32)
     for at in range(sections):
         p_out[at] = held
-        held = total * flag_in[at] * held + f_in[at]
+        held = total * f_in[at, depth : depth + 1] * held + f_in[at, 0:depth]
     spread(lambda peer: p_out.at[peer], state, 2)
+    pending.append(all_but_one(state, 2))
     state[me] = p_out[me]
+    lax.fori_loop(1, 2, forward_head, 0)
     all_but_one(state, 2).wait_recv()
 
     def state_of(buffer, h):
@@ -206,15 +233,18 @@
         return 0
 
     lax.fori_loop(0, 2, finish_outputs, 0)
+    loads[4].wait()
+    loads[5].wait()
     outputs = o[...]
     upstream = g_ref[...].astype(f32)
-    grad_norm = upstream * gain_ref[...].astype(f32)
+    grad_norm = upstream * gain_ref[...].astype(f32)[None, :]
     squares = outputs * outputs
     mixes = grad_norm * outputs
     pair_out[0:1] = jnp.sum(jnp.transpose(squares[:, 0:128] + squares[:, 128:256]), 0, keepdims=True)
     pair_out[1:2] = jnp.sum(jnp.transpose(mixes[:, 0:128] + mixes[:, 128:256]), 0, keepdims=True)
     swap = to_column(pair_out, pair_in, 3, other)
     swap.start()
+    pending.append(swap)
     swap.wait_recv()
     line = pair_out[...] + pair_in[...]
     line_out[...] = line
@@ -228,6 +258,7 @@
     lax.fori_loop(1, tiers, one_tier, 0)
     tier_part = line_in.at[pl.ds(0, tiers - 1)]
     tier_wait = to_column(tier_part, tier_part, 4, other)
+    pending.append(tier_wait)
     tier_wait.wait_recv()
     sums = line_in[0]
     for at in range(1, tiers):
@@ -257,7 +288,7 @@
     b_in[me] = b_out[me]
     gain_in[me] = gain_out[...]
     spread(lambda peer: b_out.at[peer], b_in, 5)
-    spread(lambda peer: gain_out, gain_in, 6)
+    pending.append(all_but_one(b_in, 5))
 
     def start_query(h, _):
         hi, lo = state_of(state, h)
@@ -267,14 +298,6 @@
         return 0
 
     lax.fori_loop(0, 2, start_query, 0)
-
-    all_but_one(b_in, 5).wait_recv()
-    held = jnp.zeros((depth, 128), f32)
-    for at in reversed(range(sections)):
-        c_out[at] = held
-        held = total * flag_in[at] * held + b_in[at]
-    spread(lambda peer: c_out.at[peer], carry, 7)
-    carry[me] = c_out[me]
 
     def backward_pair(h, at, past):
         ti, si = pl.ds(at * block, block), pl.ds(past * block, block)
@@ -298,12 +321,18 @@
         pairs(h, backward_pair)
         return 0
 
-    lax.fori_loop(0, 2, backward_head, 0)
-    all_but_one(gain_in, 6).wait_recv()
-    gains = gain_in[0]
-    for at in range(1, sections):
-        gains = gains + gain_in[at]
-    gg_ref[...] = gains / math.sqrt(rows * sections)
+    lax.fori_loop(0, 1, backward_head, 0)
+    all_but_one(b_in, 5).wait_recv()
+    held = jnp.zeros((depth, 128), f32)
+    for at in reversed(range(sections)):
+        c_out[at] = held
+        held = total * f_in[at, depth : depth + 1] * held + b_in[at]
+    spread(lambda peer: c_out.at[peer], carry, 7)
+    pending.append(all_but_one(carry, 7))
+    spread(lambda peer: gain_out, gain_in, 6)
+    pending.append(all_but_one(gain_in, 6))
+    carry[me] = c_out[me]
+    lax.fori_loop(1, 2, backward_head, 0)
     all_but_one(carry, 7).wait_recv()
 
     def finish(h, _):
@@ -315,14 +344,28 @@
         return 0
 
     lax.fori_loop(0, 2, finish, 0)
-    all_but_one(f_in, 0).wait_send()
-    all_but_one(flag_in, 1).wait_send()
-    all_but_one(state, 2).wait_send()
-    swap.wait_send()
-    tier_wait.wait_send()
-    all_but_one(b_in, 5).wait_send()
-    all_but_one(gain_in, 6).wait_send()
-    all_but_one(carry, 7).wait_send()
+    all_but_one(gain_in, 6).wait_recv()
+    gains = gain_in[0]
+    for at in range(1, sections):
+        gains = gains + gain_in[at]
+    gg_ref[...] = gains / math.sqrt(rows * sections)
+    for copy in pending:
+        copy.wait_send()
+
+
+def store_kernel(gq_ref, gk_ref, gv_ref, gg_ref, gq_hbm, gk_hbm, gv_hbm, gain_ref, cast, sems):
+    copies = []
+    for at, (source, target) in enumerate(
+        [(gq_ref, gq_hbm), (gk_ref, gk_hbm), (gv_ref, gv_hbm)]
+    ):
+        cast[at] = source[...].astype(bf16)
+        copy = pltpu.make_async_copy(cast.at[at], target, sems.at[at])
+        copy.start()
+        copies.append(copy)
+    gain_ref[pl.ds(0, 128)] = gg_ref[0]
+    gain_ref[pl.ds(128, 128)] = gg_ref[1]
+    for copy in copies:
+        copy.wait()
 
 
 def shards(queries, key_input, values_in, cotangent, norm_gain, decay_log, doc_starts):
@@ -332,16 +375,22 @@
     depth = width // sections
     tiers = columns // 2
     vmem = pl.BlockSpec(memory_space=pltpu.VMEM)
+    hbm = pl.BlockSpec(memory_space=pltpu.HBM)
+    smem = pl.BlockSpec(memory_space=pltpu.SMEM)
     pieces = pltpu.VMEM((sections, depth, 128), f32)
+    flagged = pltpu.VMEM((sections, depth + 1, 128), f32)
+    tokens = pltpu.VMEM((rows, width), bf16)
     outs = pl.pallas_call(
         functools.partial(kernel, sections, columns, rows, 256),
         out_shape=[jax.ShapeDtypeStruct((rows, width), f32)] * 3
         + [jax.ShapeDtypeStruct((2, 128), f32)],
-        in_specs=[vmem] * 5 + [pl.BlockSpec(memory_space=pltpu.SMEM), vmem],
+        in_specs=[hbm] * 5 + [smem, hbm],
         out_specs=[vmem] * 4,
         scratch_shapes=[
-            pltpu.VMEM((1, 128), f32), pltpu.VMEM((sections, 1, 128), f32),
-            pieces, pieces, pieces, pieces,
+            tokens, tokens, tokens, tokens,
+            pltpu.VMEM((width,), bf16), pltpu.VMEM((rows,), jnp.int32),
+            pltpu.SemaphoreType.DMA((6,)),
+            flagged, flagged, pieces, pieces,
             pieces, pieces, pieces, pieces,
             pltpu.VMEM((2, 128), f32), pltpu.VMEM((sections, 2, 128), f32),
             pltpu.VMEM((2, rows), f32), pltpu.VMEM((2, rows), f32),
@@ -350,7 +399,7 @@
             pltpu.VMEM((2, rows, rows), f32),
             pltpu.VMEM((2, rows, rows), bf16), pltpu.VMEM((2, rows, rows), bf16),
             pltpu.VMEM((rows, width), f32),
-            pltpu.VMEM((rows, width), bf16), pltpu.VMEM((rows, width), bf16),
+            tokens, tokens,
             pltpu.SemaphoreType.DMA((8,)), pltpu.SemaphoreType.DMA((8,)),
         ],
         compiler_params=pltpu.CompilerParams(
@@ -358,11 +407,26 @@
         ),
         name="layer_grads",
     )(
-        queries, key_input, values_in, cotangent, norm_gain.reshape(1, width), decay_log,
-        doc_starts.reshape(1, rows),
+        *(
+            pltpu.with_memory_space_constraint(x, pltpu.HBM)
+            for x in (queries, key_input, values_in, cotangent, norm_gain)
+        ),
+        decay_log,
+        pltpu.with_memory_space_constraint(doc_starts, pltpu.HBM),
     )
-    return (
-        outs[0].astype(bf16), outs[1].astype(bf16), outs[2].astype(bf16), outs[3].reshape(width),
+    return tuple(
+        pl.pallas_call(
+            store_kernel,
+            out_shape=[jax.ShapeDtypeStruct((rows, width), bf16)] * 3
+            + [jax.ShapeDtypeStruct((width,), f32)],
+            in_specs=[vmem] * 4,
+            out_specs=[hbm] * 3 + [vmem],
+            scratch_shapes=[
+                pltpu.VMEM((3, rows, width), bf16), pltpu.SemaphoreType.DMA((3,)),
+            ],
+            compiler_params=pltpu.CompilerParams(vmem_limit_bytes=8 * 1024 * 1024),
+            name="store_grads",
+        )(*outs)
     )
 
 

time: 68.2 us -> 59.6 us (0.87)
  local copies, waits for them, and re-layouts: 5.91 us -> 0.65 us
  other arithmetic: 2.36 us -> 0 us
  Pallas kernels: 59 us -> 58.2 us
    unnamed x11 -> x2, local copies, waits for them, and re-layouts: 4.55 us -> 0.65 us
    pallas_call x1, Pallas kernels: 59 us -> 56.6 us  [shards(): pl.pallas_call(functools.partial(kernel, sections, columns, rows, 256), o...]
    convert_element_type x3 -> x0, other arithmetic: 2.36 us -> none  [the longest x1 0.79 us: shards(): outs[0].astype(bf16)]
    pallas_call x0 -> x1, Pallas kernels: none -> 1.63 us  [shards(): pl.pallas_call(store_kernel, out_shape=[jax.ShapeDtypeStruct((rows, width...]
    reshape x2 -> x0, local copies, waits for them, and re-layouts: 1.36 us -> none  [the longest x1 0.7 us: shards(): doc_starts.reshape(1, rows)]
where the time goes in v2:
time: 59.6 us; the launch traced here: 59.5 us
  Pallas kernels  58.2 us (98%)
  local copies, waits for them, and re-layouts  0.65 us (1%)
  between operations  0.65 us (1%)
    pallas_call x1, Pallas kernels, shards(): pl.pallas_call(functools.partial(kernel, sections, columns, rows, 256), o...  56.6 us
    pallas_call x1, Pallas kernels, shards(): pl.pallas_call(store_kernel, out_shape=[jax.ShapeDtypeStruct((rows, width...  1.63 us

profile of v2, /device:TPU:1, one launch (start us, length us, event | category | flops | bytes accessed | tf_op | source)
XLA Modules:
  0.0 59.5 jit_solution(6192449913462898647)
XLA Ops:
  0.6 0.0 copy-start
  0.6 0.6 %copy-done = f32[2]{0:T(128)S(1)} copy-done((f32[2]{0:T(128)S(1)}, f32[2]{0:T(128)}, u32[]{:S(2)}) %copy-start) | copy-done | bytes 32
  1.3 56.6 %layer_grads.1 = (f32[768,256]{1,0:T(8,128)S(1)}, f32[768,256]{1,0:T(8,128)S(1)}, f32[768,256]{1,0:T(8,128)S(1)}, f32[2,128]{1,0:T(2,128)S(1)}) custom-call(bf16[768,256]{1,0:T(8,128)(2,1)} %q_hbm.1, bf16[768,256]{1,0:T(8,128)(2,1)} %k_hbm.1, bf16[768,256]{1,0:T(8,128)(2,1)} %v_hbm.1, bf16[768,256]{1,0:T(8,128)(2,1)} %g_hbm.1, bf16[256]{0:T(256)(128)(2,1)} %gain_hbm.1, ...), custom_call_target="tpu_custom_call" | custom-call | tf_op jit(solution)/shard_map/layer_grads/pallas_call | solution.py:383
  57.9 1.6 %store_grads.1 = (bf16[768,256]{1,0:T(8,128)(2,1)}, bf16[768,256]{1,0:T(8,128)(2,1)}, bf16[768,256]{1,0:T(8,128)(2,1)}, f32[256]{0:T(256)}) custom-call(f32[768,256]{1,0:T(8,128)S(1)} %get-tuple-element.8.gq_ref, f32[768,256]{1,0:T(8,128)S(1)} %get-tuple-element.9.gk_ref, f32[768,256]{1,0:T(8,128)S(1)} %get-tuple-element.10.gv_ref, ...), custom_call_target="tpu_custom_call" | custom-call | tf_op jit(solution)/shard_map/store_grads/pallas_call | solution.py:418
Async XLA Ops:
  0.6 0.7 %copy-start = (f32[2]{0:T(128)S(1)}, f32[2]{0:T(128)}, u32[]{:S(2)}) copy-start(f32[2]{0:T(128)} %decay_ref.1) | copy-start | bytes 28

commit v3 on v2

--- a/solution.py
+++ b/solution.py
@@ -41,8 +41,9 @@
 
 def kernel(
     sections, columns, rows, block,
-    q_hbm, k_hbm, v_hbm, g_hbm, gain_hbm, decay_ref, doc_hbm,
-    gq_ref, gk_ref, gv_ref, gg_ref,
+    q_hbm, k_hbm, v_hbm, g_hbm, gain_hbm, decay_hbm, doc_hbm,
+    gq_out, gk_out, gv_out, gg_ref,
+    gq_ref, gk_ref, gv_ref, decay_ref,
     q_ref, k_ref, v_ref, g_ref, gain_ref, doc_ref, local_sem,
     f_out, f_in, p_out, state,
     b_out, b_in, c_out, carry,
@@ -96,36 +97,32 @@
         part = buffer.at[pl.ds(0, sections - 1)]
         return to_section(part, part, which, (me + 1) % sections)
 
+    barrier = pltpu.get_barrier_semaphore()
+    other = z_at * 2 + (1 - x_at)
+    line_hops = sorted(range(1, tiers), key=lambda z: -min(z, tiers - z))
+
+    def line_peer(hop):
+        return ((z_at + hop) % tiers) * 2 + x_at
+
+    def greet(peer):
+        pl.semaphore_signal(barrier, inc=1, device_id=peer, device_id_type=MESH)
+
+    for hop in line_hops:
+        greet({"dp": line_peer(hop)})
+    for step in steps:
+        greet({"section": peer_at(*step)})
+    greet({"dp": other})
+
     loads = []
     for at, (source, target) in enumerate(
         [
             (doc_hbm, doc_ref), (k_hbm, k_ref), (v_hbm, v_ref),
-            (q_hbm, q_ref), (g_hbm, g_ref), (gain_hbm, gain_ref),
+            (q_hbm, q_ref), (g_hbm, g_ref), (gain_hbm, gain_ref), (decay_hbm, decay_ref),
         ]
     ):
         load = pltpu.make_async_copy(source, target, local_sem.at[at])
         load.start()
         loads.append(load)
-
-    barrier = pltpu.get_barrier_semaphore()
-
-    def greet(step, _):
-        pl.semaphore_signal(
-            barrier, inc=1, device_id={"section": (me + step) % sections}, device_id_type=MESH
-        )
-        return 0
-
-    def greet_line(step, _):
-        pl.semaphore_signal(
-            barrier, inc=1, device_id={"dp": ((z_at + step) % tiers) * 2 + x_at},
-            device_id_type=MESH,
-        )
-        return 0
-
-    lax.fori_loop(1, sections, greet, 0)
-    other = z_at * 2 + (1 - x_at)
-    pl.semaphore_signal(barrier, inc=1, device_id={"dp": other}, device_id_type=MESH)
-    lax.fori_loop(1, tiers, greet_line, 0)
 
     loads[0].wait()
     upper = (
@@ -163,12 +160,15 @@
     )
     loads[1].wait()
     loads[2].wait()
+    loads[6].wait()
     lax.fori_loop(0, 2, local_states, 0)
     f_in[me] = f_out[me]
 
     pl.semaphore_wait(barrier, sections + tiers - 1)
     spread(lambda peer: f_out.at[peer], f_in, 0)
     pending.append(all_but_one(f_in, 0))
+
+    loads[3].wait()
 
     def pairs(h, body):
         for at in range(blocks):
@@ -200,28 +200,28 @@
         else:
             o[ti, head_slice(h)] += term
 
+    rate = jnp.where(me < half, decay_ref[0], decay_ref[1])
+    total = jnp.exp(jnp.full((depth, 128), rate * rows, f32))
+    f_all, state_all = all_but_one(f_in, 0), all_but_one(state, 2)
+
     def forward_head(h, _):
         pairs(h, forward_pair)
-        return 0
-
-    loads[3].wait()
-    lax.fori_loop(0, 1, forward_head, 0)
-
-    def factors():
-        rate = jnp.where(me < half, decay_ref[0], decay_ref[1])
-        return jnp.exp(jnp.full((depth, 128), rate * rows, f32))
-
-    all_but_one(f_in, 0).wait_recv()
-    total = factors()
-    held = jnp.zeros((depth, 128), f32)
-    for at in range(sections):
-        p_out[at] = held
-        held = total * f_in[at, depth : depth + 1] * held + f_in[at, 0:depth]
-    spread(lambda peer: p_out.at[peer], state, 2)
-    pending.append(all_but_one(state, 2))
+
+        @pl.when(h == 0)
+        def _():
+            f_all.wait_recv()
+            held = jnp.zeros((depth, 128), f32)
+            for at in range(sections):
+                p_out[at] = held
+                held = total * f_in[at, depth : depth + 1] * held + f_in[at, 0:depth]
+            spread(lambda peer: p_out.at[peer], state, 2)
+
+        return 0
+
+    lax.fori_loop(0, 2, forward_head, 0)
+    pending.append(state_all)
     state[me] = p_out[me]
-    lax.fori_loop(1, 2, forward_head, 0)
-    all_but_one(state, 2).wait_recv()
+    state_all.wait_recv()
 
     def state_of(buffer, h):
         return split(buffer[pl.ds(h * half, half)].reshape(128, 128))
@@ -250,12 +250,8 @@
     line_out[...] = line
     line_in[z_at] = line
 
-    def one_tier(step, _):
-        peer = ((z_at + step) % tiers) * 2 + x_at
-        to_column(line_out, line_in.at[z_at], 4, peer).start()
-        return 0
-
-    lax.fori_loop(1, tiers, one_tier, 0)
+    for hop in line_hops:
+        to_column(line_out, line_in.at[z_at], 4, line_peer(hop)).start()
     tier_part = line_in.at[pl.ds(0, tiers - 1)]
     tier_wait = to_column(tier_part, tier_part, 4, other)
     pending.append(tier_wait)
@@ -317,30 +313,38 @@
             gk_ref[si, head_slice(h)] += key_term
             gv_ref[si, head_slice(h)] += value_term
 
+    b_all, carry_all = all_but_one(b_in, 5), all_but_one(carry, 7)
+
     def backward_head(h, _):
         pairs(h, backward_pair)
-        return 0
-
-    lax.fori_loop(0, 1, backward_head, 0)
-    all_but_one(b_in, 5).wait_recv()
-    held = jnp.zeros((depth, 128), f32)
-    for at in reversed(range(sections)):
-        c_out[at] = held
-        held = total * f_in[at, depth : depth + 1] * held + b_in[at]
-    spread(lambda peer: c_out.at[peer], carry, 7)
-    pending.append(all_but_one(carry, 7))
-    spread(lambda peer: gain_out, gain_in, 6)
+        gq_out[:, head_slice(h)] = gq_ref[:, head_slice(h)].astype(bf16)
+
+        @pl.when(h == 0)
+        def _():
+            b_all.wait_recv()
+            held = jnp.zeros((depth, 128), f32)
+            for at in reversed(range(sections)):
+                c_out[at] = held
+                held = total * f_in[at, depth : depth + 1] * held + b_in[at]
+            spread(lambda peer: c_out.at[peer], carry, 7)
+            spread(lambda peer: gain_out, gain_in, 6)
+
+        return 0
+
+    lax.fori_loop(0, 2, backward_head, 0)
+    pending.append(carry_all)
     pending.append(all_but_one(gain_in, 6))
     carry[me] = c_out[me]
-    lax.fori_loop(1, 2, backward_head, 0)
-    all_but_one(carry, 7).wait_recv()
+    carry_all.wait_recv()
 
     def finish(h, _):
         hi, lo = state_of(carry, h)
         both = nt(v_ref[:, head_slice(h)], jnp.concatenate([hi, lo], axis=0))
-        gk_ref[:, head_slice(h)] += suf[h] * (both[:, 0:128] + both[:, 128:256])
+        grads = gk_ref[:, head_slice(h)] + suf[h] * (both[:, 0:128] + both[:, 128:256])
+        gk_out[:, head_slice(h)] = grads.astype(bf16)
         both = nn(k_ref[:, head_slice(h)], wide(hi, lo))
-        gv_ref[:, head_slice(h)] += suf[h] * (both[:, 0:128] + both[:, 128:256])
+        grads = gv_ref[:, head_slice(h)] + suf[h] * (both[:, 0:128] + both[:, 128:256])
+        gv_out[:, head_slice(h)] = grads.astype(bf16)
         return 0
 
     lax.fori_loop(0, 2, finish, 0)
@@ -353,13 +357,12 @@
         copy.wait_send()
 
 
-def store_kernel(gq_ref, gk_ref, gv_ref, gg_ref, gq_hbm, gk_hbm, gv_hbm, gain_ref, cast, sems):
+def store_kernel(gq_ref, gk_ref, gv_ref, gg_ref, gq_hbm, gk_hbm, gv_hbm, gain_ref, sems):
     copies = []
     for at, (source, target) in enumerate(
         [(gq_ref, gq_hbm), (gk_ref, gk_hbm), (gv_ref, gv_hbm)]
     ):
-        cast[at] = source[...].astype(bf16)
-        copy = pltpu.make_async_copy(cast.at[at], target, sems.at[at])
+        copy = pltpu.make_async_copy(source, target, sems.at[at])
         copy.start()
         copies.append(copy)
     gain_ref[pl.ds(0, 128)] = gg_ref[0]
@@ -376,20 +379,21 @@
     tiers = columns // 2
     vmem = pl.BlockSpec(memory_space=pltpu.VMEM)
     hbm = pl.BlockSpec(memory_space=pltpu.HBM)
-    smem = pl.BlockSpec(memory_space=pltpu.SMEM)
+    sums = pltpu.VMEM((rows, width), f32)
     pieces = pltpu.VMEM((sections, depth, 128), f32)
     flagged = pltpu.VMEM((sections, depth + 1, 128), f32)
     tokens = pltpu.VMEM((rows, width), bf16)
     outs = pl.pallas_call(
         functools.partial(kernel, sections, columns, rows, 256),
-        out_shape=[jax.ShapeDtypeStruct((rows, width), f32)] * 3
+        out_shape=[jax.ShapeDtypeStruct((rows, width), bf16)] * 3
         + [jax.ShapeDtypeStruct((2, 128), f32)],
-        in_specs=[hbm] * 5 + [smem, hbm],
+        in_specs=[hbm] * 7,
         out_specs=[vmem] * 4,
         scratch_shapes=[
+            sums, sums, sums, pltpu.SMEM((2,), f32),
             tokens, tokens, tokens, tokens,
             pltpu.VMEM((width,), bf16), pltpu.VMEM((rows,), jnp.int32),
-            pltpu.SemaphoreType.DMA((6,)),
+            pltpu.SemaphoreType.DMA((7,)),
             flagged, flagged, pieces, pieces,
             pieces, pieces, pieces, pieces,
             pltpu.VMEM((2, 128), f32), pltpu.VMEM((sections, 2, 128), f32),
@@ -409,10 +413,10 @@
     )(
         *(
             pltpu.with_memory_space_constraint(x, pltpu.HBM)
-            for x in (queries, key_input, values_in, cotangent, norm_gain)
-        ),
-        decay_log,
-        pltpu.with_memory_space_constraint(doc_starts, pltpu.HBM),
+            for x in (
+                queries, key_input, values_in, cotangent, norm_gain, decay_log, doc_starts,
+            )
+        )
     )
     return tuple(
         pl.pallas_call(
@@ -421,9 +425,7 @@
             + [jax.ShapeDtypeStruct((width,), f32)],
             in_specs=[vmem] * 4,
             out_specs=[hbm] * 3 + [vmem],
-            scratch_shapes=[
-                pltpu.VMEM((3, rows, width), bf16), pltpu.SemaphoreType.DMA((3,)),
-            ],
+            scratch_shapes=[pltpu.SemaphoreType.DMA((3,))],
             compiler_params=pltpu.CompilerParams(vmem_limit_bytes=8 * 1024 * 1024),
             name="store_grads",
         )(*outs)

time: 59.6 us -> 57.2 us (0.960)
  Pallas kernels: 58.2 us -> 56.4 us
  local copies, waits for them, and re-layouts: 0.65 us -> 0 us
    pallas_call x1, Pallas kernels: 56.6 us -> 54.8 us  [shards(): pl.pallas_call(functools.partial(kernel, sections, columns, rows, 256), o...]
    unnamed x2 -> x0, local copies, waits for them, and re-layouts: 0.65 us -> none
where the time goes in v3:
time: 57.2 us; the launch traced here: 57.1 us
  Pallas kernels  56.4 us (99%)
  between operations  0.64 us (1%)
    pallas_call x1, Pallas kernels, shards(): pl.pallas_call(functools.partial(kernel, sections, columns, rows, 256), o...  54.8 us
    pallas_call x1, Pallas kernels, shards(): pl.pallas_call(store_kernel, out_shape=[jax.ShapeDtypeStruct((rows, width...  1.59 us

profile of v3, /device:TPU:1, one launch (start us, length us, event | category | flops | bytes accessed | tf_op | source)
XLA Modules:
  0.0 57.1 jit_solution(11055928536816935598)
XLA Ops:
  0.6 54.8 %layer_grads.1 = (bf16[768,256]{1,0:T(8,128)(2,1)S(1)}, bf16[768,256]{1,0:T(8,128)(2,1)S(1)}, bf16[768,256]{1,0:T(8,128)(2,1)S(1)}, f32[2,128]{1,0:T(2,128)S(1)}) custom-call(bf16[768,256]{1,0:T(8,128)(2,1)} %q_hbm.1, bf16[768,256]{1,0:T(8,128)(2,1)} %k_hbm.1, bf16[768,256]{1,0:T(8,128)(2,1)} %v_hbm.1, bf16[768,256]{1,0:T(8,128)(2,1)} %g_hbm.1, ...), custom_call_target="tpu_custom_call" | custom-call | tf_op jit(solution)/shard_map/layer_grads/pallas_call | solution.py:386
  55.5 1.6 %store_grads.1 = (bf16[768,256]{1,0:T(8,128)(2,1)}, bf16[768,256]{1,0:T(8,128)(2,1)}, bf16[768,256]{1,0:T(8,128)(2,1)}, f32[256]{0:T(256)}) custom-call(bf16[768,256]{1,0:T(8,128)(2,1)S(1)} %get-tuple-element.8.gq_ref, bf16[768,256]{1,0:T(8,128)(2,1)S(1)} %get-tuple-element.9.gk_ref, bf16[768,256]{1,0:T(8,128)(2,1)S(1)} %get-tuple-element.10.gv_ref, ...), custom_call_target="tpu_custom_call" | custom-call | tf_op jit(solution)/shard_map/store_grads/pallas_call | solution.py:422

commit v4 on v3

--- a/solution.py
+++ b/solution.py
@@ -42,14 +42,14 @@
 def kernel(
     sections, columns, rows, block,
     q_hbm, k_hbm, v_hbm, g_hbm, gain_hbm, decay_hbm, doc_hbm,
-    gq_out, gk_out, gv_out, gg_ref,
-    gq_ref, gk_ref, gv_ref, decay_ref,
-    q_ref, k_ref, v_ref, g_ref, gain_ref, doc_ref, local_sem,
+    gq_out, gk_ref, gv_ref, gg_ref, carry_out, suf, k_ref, v_ref,
+    gq_ref, decay_ref,
+    q_ref, g_ref, gain_ref, doc_ref, local_sem,
     f_out, f_in, p_out, state,
     b_out, b_in, c_out, carry,
     gain_out, gain_in,
-    pair_out, pair_in, line_out, line_in,
-    pre, suf, mask, s_hi, s_lo, o, d_hi, d_lo,
+    pair_out, near_in, line_out, far_in, turned,
+    pre, mask, s_hi, s_lo, o, d_hi, d_lo,
     send_sem, recv_sem,
 ):
     me = lax.axis_index("section")
@@ -98,20 +98,23 @@
         return to_section(part, part, which, (me + 1) % sections)
 
     barrier = pltpu.get_barrier_semaphore()
-    other = z_at * 2 + (1 - x_at)
-    line_hops = sorted(range(1, tiers), key=lambda z: -min(z, tiers - z))
-
-    def line_peer(hop):
-        return ((z_at + hop) % tiers) * 2 + x_at
+    reach = 3 if tiers % 3 == 0 else 1
+    near = [(z, 1) for z in (1, tiers - 1)[: reach - 1]] + [(0, 1)]
+    near += [(z, 0) for z in (1, tiers - 1)[: reach - 1]]
+    far = sorted(range(reach, tiers, reach), key=lambda z: -min(z, tiers - z))
+
+    def line_peer(z, x):
+        return ((z_at + z) % tiers) * 2 + (x_at + x) % 2
 
     def greet(peer):
         pl.semaphore_signal(barrier, inc=1, device_id=peer, device_id_type=MESH)
 
-    for hop in line_hops:
-        greet({"dp": line_peer(hop)})
+    for z in far:
+        greet({"dp": line_peer(z, 0)})
     for step in steps:
         greet({"section": peer_at(*step)})
-    greet({"dp": other})
+    for z, x in near:
+        greet({"dp": line_peer(z, x)})
 
     loads = []
     for at, (source, target) in enumerate(
@@ -164,7 +167,7 @@
     lax.fori_loop(0, 2, local_states, 0)
     f_in[me] = f_out[me]
 
-    pl.semaphore_wait(barrier, sections + tiers - 1)
+    pl.semaphore_wait(barrier, sections - 1 + len(near) + len(far))
     spread(lambda peer: f_out.at[peer], f_in, 0)
     pending.append(all_but_one(f_in, 0))
 
@@ -242,23 +245,32 @@
     mixes = grad_norm * outputs
     pair_out[0:1] = jnp.sum(jnp.transpose(squares[:, 0:128] + squares[:, 128:256]), 0, keepdims=True)
     pair_out[1:2] = jnp.sum(jnp.transpose(mixes[:, 0:128] + mixes[:, 128:256]), 0, keepdims=True)
-    swap = to_column(pair_out, pair_in, 3, other)
-    swap.start()
-    pending.append(swap)
-    swap.wait_recv()
-    line = pair_out[...] + pair_in[...]
-    line_out[...] = line
-    line_in[z_at] = line
-
-    for hop in line_hops:
-        to_column(line_out, line_in.at[z_at], 4, line_peer(hop)).start()
-    tier_part = line_in.at[pl.ds(0, tiers - 1)]
-    tier_wait = to_column(tier_part, tier_part, 4, other)
-    pending.append(tier_wait)
-    tier_wait.wait_recv()
-    sums = line_in[0]
-    for at in range(1, tiers):
-        sums = sums + line_in[at]
+    def exchange(source, target, which, offsets):
+        for at, (z, x) in enumerate(offsets):
+            to_column(source, target.at[at], which, line_peer(z, x)).start()
+        part = target.at[pl.ds(0, len(offsets))]
+        whole = to_column(part, part, which, line_peer(*offsets[0]))
+        pending.append(whole)
+        return whole
+
+    near_all = exchange(pair_out, near_in, 3, near)
+
+    def turn_queries(h, _):
+        hi, lo = split(jnp.transpose(pre[h] * q_ref[:, head_slice(h)].astype(f32)))
+        turned[h, 0:128] = hi
+        turned[h, 128:256] = lo
+        return 0
+
+    lax.fori_loop(0, 2, turn_queries, 0)
+    near_all.wait_recv()
+    sums = pair_out[...]
+    for at in range(len(near)):
+        sums = sums + near_in[at]
+    if far:
+        line_out[...] = sums
+        exchange(line_out, far_in, 4, [(z, 0) for z in far]).wait_recv()
+        for at in range(len(far)):
+            sums = sums + far_in[at]
     scale = lax.rsqrt(sums[0:1] / features + epsilon)
     mixed = scale * sums[1:2] / features
     scale = column(scale)
@@ -274,8 +286,7 @@
     gain_out[1:2] = gains[:, 128:256]
 
     def backward_states(h, _):
-        hi, lo = split(pre[h] * q_ref[:, head_slice(h)].astype(f32))
-        four = tn(wide(hi, lo), wide(d_hi[:, head_slice(h)], d_lo[:, head_slice(h)]))
+        four = nn(turned[h], wide(d_hi[:, head_slice(h)], d_lo[:, head_slice(h)]))
         top = four[0:128] + four[128:256]
         b_out[pl.ds(h * half, half)] = (top[:, 0:128] + top[:, 128:256]).reshape(half, depth, 128)
         return 0
@@ -337,17 +348,7 @@
     carry[me] = c_out[me]
     carry_all.wait_recv()
 
-    def finish(h, _):
-        hi, lo = state_of(carry, h)
-        both = nt(v_ref[:, head_slice(h)], jnp.concatenate([hi, lo], axis=0))
-        grads = gk_ref[:, head_slice(h)] + suf[h] * (both[:, 0:128] + both[:, 128:256])
-        gk_out[:, head_slice(h)] = grads.astype(bf16)
-        both = nn(k_ref[:, head_slice(h)], wide(hi, lo))
-        grads = gv_ref[:, head_slice(h)] + suf[h] * (both[:, 0:128] + both[:, 128:256])
-        gv_out[:, head_slice(h)] = grads.astype(bf16)
-        return 0
-
-    lax.fori_loop(0, 2, finish, 0)
+    carry_out[...] = carry[...]
     all_but_one(gain_in, 6).wait_recv()
     gains = gain_in[0]
     for at in range(1, sections):
@@ -357,18 +358,32 @@
         copy.wait_send()
 
 
-def store_kernel(gq_ref, gk_ref, gv_ref, gg_ref, gq_hbm, gk_hbm, gv_hbm, gain_ref, sems):
-    copies = []
-    for at, (source, target) in enumerate(
-        [(gq_ref, gq_hbm), (gk_ref, gk_hbm), (gv_ref, gv_hbm)]
-    ):
-        copy = pltpu.make_async_copy(source, target, sems.at[at])
-        copy.start()
-        copies.append(copy)
+def store_kernel(
+    gq_ref, gk_ref, gv_ref, gg_ref, carry, suf, k_ref, v_ref,
+    gq_hbm, gk_hbm, gv_hbm, gain_ref, gk_cast, gv_cast, sems,
+):
+    half = carry.shape[0] // 2
+    first = pltpu.make_async_copy(gq_ref, gq_hbm, sems.at[0])
+    first.start()
+    heads = [slice(h * 128, h * 128 + 128) for h in range(2)]
+    states = [split(carry[h * half : h * half + half].reshape(128, 128)) for h in range(2)]
+    for h in range(2):
+        both = nt(v_ref[:, heads[h]], jnp.concatenate(states[h], axis=0))
+        grads = gk_ref[:, heads[h]] + suf[h] * (both[:, 0:128] + both[:, 128:256])
+        gk_cast[:, heads[h]] = grads.astype(bf16)
+    second = pltpu.make_async_copy(gk_cast, gk_hbm, sems.at[1])
+    second.start()
+    for h in range(2):
+        both = nn(k_ref[:, heads[h]], wide(*states[h]))
+        grads = gv_ref[:, heads[h]] + suf[h] * (both[:, 0:128] + both[:, 128:256])
+        gv_cast[:, heads[h]] = grads.astype(bf16)
+    third = pltpu.make_async_copy(gv_cast, gv_hbm, sems.at[2])
+    third.start()
     gain_ref[pl.ds(0, 128)] = gg_ref[0]
     gain_ref[pl.ds(128, 128)] = gg_ref[1]
-    for copy in copies:
-        copy.wait()
+    first.wait()
+    second.wait()
+    third.wait()
 
 
 def shards(queries, key_input, values_in, cotangent, norm_gain, decay_log, doc_starts):
@@ -385,21 +400,30 @@
     tokens = pltpu.VMEM((rows, width), bf16)
     outs = pl.pallas_call(
         functools.partial(kernel, sections, columns, rows, 256),
-        out_shape=[jax.ShapeDtypeStruct((rows, width), bf16)] * 3
-        + [jax.ShapeDtypeStruct((2, 128), f32)],
+        out_shape=[
+            jax.ShapeDtypeStruct((rows, width), bf16),
+            jax.ShapeDtypeStruct((rows, width), f32),
+            jax.ShapeDtypeStruct((rows, width), f32),
+            jax.ShapeDtypeStruct((2, 128), f32),
+            jax.ShapeDtypeStruct((sections, depth, 128), f32),
+            jax.ShapeDtypeStruct((2, rows, 128), f32),
+            jax.ShapeDtypeStruct((rows, width), bf16),
+            jax.ShapeDtypeStruct((rows, width), bf16),
+        ],
         in_specs=[hbm] * 7,
-        out_specs=[vmem] * 4,
+        out_specs=[vmem] * 8,
         scratch_shapes=[
-            sums, sums, sums, pltpu.SMEM((2,), f32),
-            tokens, tokens, tokens, tokens,
+            sums, pltpu.SMEM((2,), f32),
+            tokens, tokens,
             pltpu.VMEM((width,), bf16), pltpu.VMEM((rows,), jnp.int32),
             pltpu.SemaphoreType.DMA((7,)),
             flagged, flagged, pieces, pieces,
             pieces, pieces, pieces, pieces,
             pltpu.VMEM((2, 128), f32), pltpu.VMEM((sections, 2, 128), f32),
-            pltpu.VMEM((2, rows), f32), pltpu.VMEM((2, rows), f32),
+            pltpu.VMEM((2, rows), f32), pltpu.VMEM((5, 2, rows), f32),
             pltpu.VMEM((2, rows), f32), pltpu.VMEM((tiers, 2, rows), f32),
-            pltpu.VMEM((2, rows, 128), f32), pltpu.VMEM((2, rows, 128), f32),
+            pltpu.VMEM((2, 256, rows), bf16),
+            pltpu.VMEM((2, rows, 128), f32),
             pltpu.VMEM((2, rows, rows), f32),
             pltpu.VMEM((2, rows, rows), bf16), pltpu.VMEM((2, rows, rows), bf16),
             pltpu.VMEM((rows, width), f32),
@@ -423,9 +447,9 @@
             store_kernel,
             out_shape=[jax.ShapeDtypeStruct((rows, width), bf16)] * 3
             + [jax.ShapeDtypeStruct((width,), f32)],
-            in_specs=[vmem] * 4,
+            in_specs=[vmem] * 8,
             out_specs=[hbm] * 3 + [vmem],
-            scratch_shapes=[pltpu.SemaphoreType.DMA((3,))],
+            scratch_shapes=[tokens, tokens, pltpu.SemaphoreType.DMA((3,))],
             compiler_params=pltpu.CompilerParams(vmem_limit_bytes=8 * 1024 * 1024),
             name="store_grads",
         )(*outs)

time: 57.2 us -> 58.3 us (1.019)
  Pallas kernels: 56.4 us -> 57.5 us
    pallas_call x1, Pallas kernels: 54.8 us -> 55.4 us  [shards(): pl.pallas_call(functools.partial(kernel, sections, columns, rows, 256), o...]
where the time goes in v4:
time: 58.3 us; the launch traced here: 58.1 us
  Pallas kernels  57.5 us (99%)
  between operations  0.64 us (1%)
    pallas_call x1, Pallas kernels, shards(): pl.pallas_call(functools.partial(kernel, sections, columns, rows, 256), o...  55.4 us
    pallas_call x1, Pallas kernels, shards(): pl.pallas_call(store_kernel, out_shape=[jax.ShapeDtypeStruct((rows, width...  2.07 us

profile of v4, /device:TPU:1, one launch (start us, length us, event | category | flops | bytes accessed | tf_op | source)
XLA Modules:
  0.0 58.1 jit_solution(14637497986681662925)
XLA Ops:
  0.6 55.4 %layer_grads.1 = (bf16[768,256]{1,0:T(8,128)(2,1)S(1)}, f32[768,256]{1,0:T(8,128)S(1)}, f32[768,256]{1,0:T(8,128)S(1)}, f32[2,128]{1,0:T(2,128)S(1)}, f32[32,8,1...) custom-call(bf16[768,256]{1,0:T(8,128)(2,1)} %q_hbm.1, ...), custom_call_target="tpu_custom_call" | custom-call | tf_op jit(solution)/shard_map/layer_grads/pallas_call | solution.py:401
  56.1 2.1 %store_grads.1 = (bf16[768,256]{1,0:T(8,128)(2,1)}, bf16[768,256]{1,0:T(8,128)(2,1)}, bf16[768,256]{1,0:T(8,128)(2,1)}, f32[256]{0:T(256)}) custom-call(bf16[768,256]{1,0:T(8,128)(2,1)S(1)} %get-tuple-element.12.gq_ref, f32[768,256]{1,0:T(8,128)S(1)} %get-tuple-element.13.gk_ref, f32[768,256]{1,0:T(8,128)S(1)} %get-tuple-element.14.gv_ref, ...), custom_call_target="tpu_custom_call" | custom-call | tf_op jit(solution)/shard_map/store_grads/pallas_call | solution.py:446

commit v5 on v3

--- a/solution.py
+++ b/solution.py
@@ -48,7 +48,7 @@
     f_out, f_in, p_out, state,
     b_out, b_in, c_out, carry,
     gain_out, gain_in,
-    pair_out, pair_in, line_out, line_in,
+    pair_out, line_in, turned, ready,
     pre, suf, mask, s_hi, s_lo, o, d_hi, d_lo,
     send_sem, recv_sem,
 ):
@@ -165,6 +165,7 @@
     f_in[me] = f_out[me]
 
     pl.semaphore_wait(barrier, sections + tiers - 1)
+    pl.semaphore_signal(ready, inc=1, device_id={"dp": other}, device_id_type=MESH)
     spread(lambda peer: f_out.at[peer], f_in, 0)
     pending.append(all_but_one(f_in, 0))
 
@@ -242,22 +243,27 @@
     mixes = grad_norm * outputs
     pair_out[0:1] = jnp.sum(jnp.transpose(squares[:, 0:128] + squares[:, 128:256]), 0, keepdims=True)
     pair_out[1:2] = jnp.sum(jnp.transpose(mixes[:, 0:128] + mixes[:, 128:256]), 0, keepdims=True)
-    swap = to_column(pair_out, pair_in, 3, other)
-    swap.start()
-    pending.append(swap)
-    swap.wait_recv()
-    line = pair_out[...] + pair_in[...]
-    line_out[...] = line
-    line_in[z_at] = line
-
-    for hop in line_hops:
-        to_column(line_out, line_in.at[z_at], 4, line_peer(hop)).start()
-    tier_part = line_in.at[pl.ds(0, tiers - 1)]
-    tier_wait = to_column(tier_part, tier_part, 4, other)
-    pending.append(tier_wait)
-    tier_wait.wait_recv()
-    sums = line_in[0]
-    for at in range(1, tiers):
+    offsets = sorted(
+        [(z, x) for z in range(tiers) for x in range(2) if (z, x) != (0, 0)],
+        key=lambda hop: -(min(hop[0], tiers - hop[0]) + 2 * hop[1]),
+    )
+    pl.semaphore_wait(ready, 1)
+    for at, (z, x) in enumerate(offsets):
+        peer = ((z_at + z) % tiers) * 2 + (x_at + x) % 2
+        to_column(pair_out, line_in.at[at], 4, peer).start()
+    line_all = to_column(line_in, line_in, 4, other)
+    pending.append(line_all)
+
+    def turn_queries(h, _):
+        hi, lo = split(jnp.transpose(pre[h] * q_ref[:, head_slice(h)].astype(f32)))
+        turned[h, 0:128] = hi
+        turned[h, 128:256] = lo
+        return 0
+
+    lax.fori_loop(0, 2, turn_queries, 0)
+    line_all.wait_recv()
+    sums = pair_out[...]
+    for at in range(len(offsets)):
         sums = sums + line_in[at]
     scale = lax.rsqrt(sums[0:1] / features + epsilon)
     mixed = scale * sums[1:2] / features
@@ -274,8 +280,7 @@
     gain_out[1:2] = gains[:, 128:256]
 
     def backward_states(h, _):
-        hi, lo = split(pre[h] * q_ref[:, head_slice(h)].astype(f32))
-        four = tn(wide(hi, lo), wide(d_hi[:, head_slice(h)], d_lo[:, head_slice(h)]))
+        four = nn(turned[h], wide(d_hi[:, head_slice(h)], d_lo[:, head_slice(h)]))
         top = four[0:128] + four[128:256]
         b_out[pl.ds(h * half, half)] = (top[:, 0:128] + top[:, 128:256]).reshape(half, depth, 128)
         return 0
@@ -397,8 +402,8 @@
             flagged, flagged, pieces, pieces,
             pieces, pieces, pieces, pieces,
             pltpu.VMEM((2, 128), f32), pltpu.VMEM((sections, 2, 128), f32),
-            pltpu.VMEM((2, rows), f32), pltpu.VMEM((2, rows), f32),
-            pltpu.VMEM((2, rows), f32), pltpu.VMEM((tiers, 2, rows), f32),
+            pltpu.VMEM((2, rows), f32), pltpu.VMEM((columns - 1, 2, rows), f32),
+            pltpu.VMEM((2, 256, rows), bf16), pltpu.SemaphoreType.REGULAR,
             pltpu.VMEM((2, rows, 128), f32), pltpu.VMEM((2, rows, 128), f32),
             pltpu.VMEM((2, rows, rows), f32),
             pltpu.VMEM((2, rows, rows), bf16), pltpu.VMEM((2, rows, rows), bf16),

time: 57.2 us -> 56.6 us (0.990)
  Pallas kernels: 56.4 us -> 55.8 us
    pallas_call x1, Pallas kernels: 54.8 us -> 54.2 us  [shards(): pl.pallas_call(functools.partial(kernel, sections, columns, rows, 256), o...]
where the time goes in v5:
time: 56.6 us; the launch traced here: 56.4 us
  Pallas kernels  55.8 us (99%)
  between operations  0.64 us (1%)
    pallas_call x1, Pallas kernels, shards(): pl.pallas_call(functools.partial(kernel, sections, columns, rows, 256), o...  54.2 us
    pallas_call x1, Pallas kernels, shards(): pl.pallas_call(store_kernel, out_shape=[jax.ShapeDtypeStruct((rows, width...  1.59 us

profile of v5, /device:TPU:1, one launch (start us, length us, event | category | flops | bytes accessed | tf_op | source)
XLA Modules:
  0.0 56.4 jit_solution(14185999031487954169)
XLA Ops:
  0.6 54.2 %layer_grads.1 = (bf16[768,256]{1,0:T(8,128)(2,1)S(1)}, bf16[768,256]{1,0:T(8,128)(2,1)S(1)}, bf16[768,256]{1,0:T(8,128)(2,1)S(1)}, f32[2,128]{1,0:T(2,128)S(1)}) custom-call(bf16[768,256]{1,0:T(8,128)(2,1)} %q_hbm.1, bf16[768,256]{1,0:T(8,128)(2,1)} %k_hbm.1, bf16[768,256]{1,0:T(8,128)(2,1)} %v_hbm.1, bf16[768,256]{1,0:T(8,128)(2,1)} %g_hbm.1, ...), custom_call_target="tpu_custom_call" | custom-call | tf_op jit(solution)/shard_map/layer_grads/pallas_call | solution.py:391
  54.8 1.6 %store_grads.1 = (bf16[768,256]{1,0:T(8,128)(2,1)}, bf16[768,256]{1,0:T(8,128)(2,1)}, bf16[768,256]{1,0:T(8,128)(2,1)}, f32[256]{0:T(256)}) custom-call(bf16[768,256]{1,0:T(8,128)(2,1)S(1)} %get-tuple-element.8.gq_ref, bf16[768,256]{1,0:T(8,128)(2,1)S(1)} %get-tuple-element.9.gk_ref, bf16[768,256]{1,0:T(8,128)(2,1)S(1)} %get-tuple-element.10.gv_ref, ...), custom_call_target="tpu_custom_call" | custom-call | tf_op jit(solution)/shard_map/store_grads/pallas_call | solution.py:427
